TPU v7x, 32 devices: a whole 2x2x4 slice. The times are simulated.
32 devices in a mesh: blk: 8 (over z, y), wide: 4 (over x, core).
Axes of the slice: x: 2, y: 2, z: 4, core: 2. Of those that a mesh axis runs over, the one named last changes fastest.
Arguments:
- query_rows: bfloat16 [4, 1024, 1536], P('wide', 'blk'), may hold values from -40 to 40
- key_rows: bfloat16 [4, 1024, 1536], P('wide', 'blk'), may hold values from -6 to 6
- value_rows: bfloat16 [4, 1024, 1536], P('wide', 'blk'), may hold values from -6 to 6
- patch_index: int32 [4, 1024], P('wide', 'blk'), may hold values from 0 to 4095, as said below
- live_count: int32 [4, 8], P('wide', 'blk'), may hold values from 64 to 128, as said below
- slopes: float32 [12], replicated, may hold values from 0.003 to 0.15
- out_weight: bfloat16 [1536, 1536], P('wide'), may hold values from -0.15625 to 0.15625
- out_grad: bfloat16 [4, 1024, 1536], P('wide', 'blk'), may hold values from -6 to 6
Outputs:
- layer_out: bfloat16 [4, 1024, 1536], P('wide', 'blk')
- grad_query: bfloat16 [4, 1024, 1536], P('wide', 'blk')
- grad_key: bfloat16 [4, 1024, 1536], P('wide', 'blk')
- grad_value: bfloat16 [4, 1024, 1536], P('wide', 'blk')
- grad_weight: float32 [1536, 1536], P('wide')
Inputs may be any that keep to these rules, and one draw needn't show every extreme that they name: `patch_index`: within a slab b, the slots hold distinct patch numbers of the range b * 512 to (b + 1) * 512 - 1 in increasing order; slots beyond the live count hold such numbers too. `live_count`: every crop has a slab with exactly 128 live slots; the live slots of a slab are its first ones.
All inputs are finite; a program needn't handle non-finite values.
Results may differ from a plain program's by a relative error of at most 0.015.
Values may be sent and summed in bfloat16 or wider, within the bound.
A program may use at most 128 MiB of HBM per device.

v0:
```python
import jax
import jax.numpy as jnp
from jax import lax
from jax.sharding import PartitionSpec as P

HEADS = 12
HEAD_DIM = 128
SIDE = 32


MASKED = -1e30


def coordinates(index):
    return (index % SIDE, index // SIDE % SIDE, index // (SIDE * SIDE))


def spacing(row_index, col_index):
    row_x, row_y, row_z = coordinates(row_index)
    col_x, col_y, col_z = coordinates(col_index)
    distance = (
        jnp.abs(row_x[:, None] - col_x[None, :])
        + jnp.abs(row_y[:, None] - col_y[None, :])
        + jnp.abs(row_z[:, None] - col_z[None, :])
    )
    return distance.astype(jnp.float32)


def biased_scores(query_heads, key_heads, row_index, col_index, key_live, slopes):
    scaling = HEAD_DIM ** (-0.5)
    scores = (
        jnp.einsum("qhd,khd->hqk", query_heads, key_heads, preferred_element_type=jnp.float32)
        * scaling
    )
    scores = scores - slopes[:, None, None] * spacing(row_index, col_index)[None]
    return jnp.where(key_live[None, None, :], scores, MASKED)


def body(query_rows, key_rows, value_rows, patch_index, live_count, slopes, out_weight, out_grad):
    slot_count = query_rows.shape[1]
    inner_width = query_rows.shape[2]
    blocks = lax.axis_size("blk")
    extent = slot_count * blocks
    scaling = HEAD_DIM ** (-0.5)
    key_all, value_all, index_all, count_all = (
        lax.all_gather(key_rows, "blk", axis=1, tiled=True),
        lax.all_gather(value_rows, "blk", axis=1, tiled=True),
        lax.all_gather(patch_index, "blk", axis=1, tiled=True),
        lax.all_gather(live_count, "blk", axis=1, tiled=True),
    )
    weight_all = lax.all_gather(out_weight, "wide", axis=0, tiled=True)
    position = jnp.arange(extent, dtype=jnp.int32)
    key_live = position % slot_count < jnp.repeat(count_all[0], slot_count)
    query_live = jnp.arange(slot_count, dtype=jnp.int32) < live_count[0, 0]
    query_heads = query_rows[0].reshape(slot_count, HEADS, HEAD_DIM)
    key_heads = key_all[0].reshape(extent, HEADS, HEAD_DIM)
    value_heads = value_all[0].reshape(extent, HEADS, HEAD_DIM)
    scores = biased_scores(query_heads, key_heads, patch_index[0], index_all[0], key_live, slopes)
    row_max = jnp.max(scores, axis=2, keepdims=True)
    row_lse = row_max + jnp.log(jnp.sum(jnp.exp(scores - row_max), axis=2, keepdims=True))
    attn_prob = jnp.exp(scores - row_lse)
    prob_low = attn_prob.astype(jnp.bfloat16)
    attended = jnp.einsum(
        "hqk,khd->qhd", prob_low, value_heads, preferred_element_type=jnp.float32
    ).reshape(slot_count, inner_width)
    attended = jnp.where(query_live[:, None], attended, 0.0).astype(jnp.bfloat16)
    layer_out = jnp.dot(attended, weight_all, preferred_element_type=jnp.float32).astype(
        jnp.bfloat16
    )
    grad_att = jnp.einsum("qo,io->qi", out_grad[0], weight_all, preferred_element_type=jnp.float32)
    grad_att = jnp.where(query_live[:, None], grad_att, 0.0).astype(jnp.bfloat16)
    grad_heads = grad_att.reshape(slot_count, HEADS, HEAD_DIM)
    grad_prob = jnp.einsum(
        "qhd,khd->hqk", grad_heads, value_heads, preferred_element_type=jnp.float32
    )
    row_delta = jnp.sum(attn_prob * grad_prob, axis=2, keepdims=True)
    grad_score = (attn_prob * (grad_prob - row_delta)).astype(jnp.bfloat16)
    grad_query = (
        jnp.einsum("hqk,khd->qhd", grad_score, key_heads, preferred_element_type=jnp.float32)
        * scaling
    )
    grad_query = grad_query.reshape(slot_count, inner_width).astype(jnp.bfloat16)
    key_part = (
        jnp.einsum("hqk,qhd->khd", grad_score, query_heads, preferred_element_type=jnp.float32)
        * scaling
    )
    value_part = jnp.einsum(
        "hqk,qhd->khd", prob_low, grad_heads, preferred_element_type=jnp.float32
    )
    stacked = lax.psum_scatter(
        jnp.concatenate(
            [
                key_part.reshape(slot_count * lax.axis_size("blk"), inner_width),
                value_part.reshape(slot_count * lax.axis_size("blk"), inner_width),
            ],
            axis=1,
        ).astype(jnp.bfloat16),
        "blk",
        scatter_dimension=0,
        tiled=True,
    ).astype(jnp.float32)
    grad_key = stacked[:, :inner_width]
    grad_value = stacked[:, inner_width:]
    weight_share = lax.psum_scatter(
        jnp.einsum("qi,qo->io", attended, out_grad[0], preferred_element_type=jnp.float32).astype(
            jnp.bfloat16
        ),
        "wide",
        scatter_dimension=0,
        tiled=True,
    )
    grad_weight = lax.psum(weight_share, "blk").astype(jnp.float32)
    return (
        layer_out[None],
        grad_query[None],
        grad_key.astype(jnp.bfloat16)[None],
        grad_value.astype(jnp.bfloat16)[None],
        grad_weight,
    )


def solution(mesh):
    placed = (
        P("wide", "blk", None),
        P("wide", "blk", None),
        P("wide", "blk", None),
        P("wide", "blk"),
        P("wide", "blk"),
        P(),
        P("wide", None),
        P("wide", "blk", None),
    )
    return jax.shard_map(
        body,
        mesh=mesh,
        in_specs=placed,
        out_specs=(
            P("wide", "blk", None),
            P("wide", "blk", None),
            P("wide", "blk", None),
            P("wide", "blk", None),
            P("wide", None),
        ),
        check_vma=False,
    )
```

profile of v0, /device:TPU:0, one launch (start us, length us, event | category | flops | bytes accessed | tf_op | source)
XLA Modules:
  0.0 438.7 jit_solution(17372420992421060902)
XLA Ops:
  7.2 0.0 copy-start
  7.2 0.0 copy-start.5
  7.2 0.0 all-gather.6.cloned.1.call-start
  7.2 0.7 all-gather.6.cloned.1.call-update
  7.9 0.0 all-gather.4.cloned.1.call-start
  8.0 1.9 copy.25
  9.9 0.0 all-gather.4.cloned.1.call-update
  9.9 0.0 all-gather.8.cloned.1.call-start
  10.0 0.7 all-gather.8.cloned.1.call-update
  10.6 0.0 reduce-scatter.5.cloned.1.call-start
  11.3 1.2 dynamic-slice
  12.6 0.7 bitcast_dynamic-update-slice_fusion
  13.3 13.2 %all-reduce = s32[8]{0:T(128)S(1)} all-reduce(s32[8]{0:T(128)S(1)} %bitcast_dynamic-update-slice_fusion), channel_id=1, replica_groups=mesh['blk'=8,'wide'=4] {'blk'}, use_global_device_ids=true, to_apply=%add | all-reduce | flops 8 | bytes 64
  26.5 1.9 copy.24
  28.4 17.8 %all_gather.17 = s32[1,1024]{1,0:T(1,128)S(1)} all-gather(s32[1,128]{1,0:T(1,128)} %param.11), channel_id=1, replica_groups=mesh['blk'=8,'wide'=4] {'blk'}, dimensions={1}, use_global_device_ids=true | all-gather | bytes 4608 | tf_op jit(solution)/shard_map/all_gather | solution.py:48
  46.2 0.1 fusion.12
  46.3 0.7 and_select_fusion.7
  47.0 0.1 and_select_fusion.1
  47.1 1.1 add_convert_fusion
  48.2 25.3 %all-gather.6.cloned.1.call-done = bf16[1,1024,1536]{2,1,0:T(8,128)(2,1)} async-done(((bf16[1,128,1536]{2,1,0:T(8,128)(2,1)}), bf16[1,1024,1536]{2,1,0:T(8,128)(2,1)}) %all-gather.6.cloned.1.call-update) | async-done | bytes 3145744 | tf_op jit(solution)/shard_map/all_gather | solution.py:47
  73.5 3.2 copy.28
  76.6 0.0 copy-start.3
  76.7 61.1 %all-gather.4.cloned.1.call-done = bf16[1,1024,1536]{1,2,0:T(8,128)(2,1)} async-done(((bf16[1,128,1536]{1,2,0:T(8,128)(2,1)}), bf16[1,1024,1536]{1,2,0:T(8,128)(2,1)}) %all-gather.4.cloned.1.call-update) | async-done | bytes 3145744 | tf_op jit(solution)/shard_map/all_gather | solution.py:46
  137.8 0.0 copy-done.5
  137.8 4.0 fusion.19
  141.8 0.0 copy-start.1
  141.8 1.5 exponential_reduce_fusion
  143.3 0.0 copy-done.3
  143.3 2.2 fusion.7
  145.5 0.0 copy-done.1
  145.5 0.0 copy-done
  145.5 3.5 convolution_convert_fusion
  149.0 0.0 reduce-scatter.5.cloned.1.call-update
  149.0 0.0 all-reduce.3.cloned.1.call-start
  149.1 25.9 %all-gather.8.cloned.1.call-done = bf16[1536,1536]{1,0:T(8,128)(2,1)} async-done(((bf16[384,1536]{1,0:T(8,128)(2,1)}), bf16[1536,1536]{1,0:T(8,128)(2,1)}) %all-gather.8.cloned.1.call-update) | async-done | bytes 4718608 | tf_op jit(solution)/shard_map/all_gather | solution.py:51
  175.0 4.0 fusion.1
  179.0 0.0 slice-start
  179.0 0.2 copy.30
  179.3 0.0 copy-start.4
  179.3 0.0 slice-start.1
  179.3 6.4 %multiply_reduce_fusion = (f32[12,128]{1,0:T(8,128)S(1)}, f32[12,128,1024]{2,1,0:T(8,128)S(1)}) fusion(f32[12,128,1024]{2,1,0:T(8,128)} %copy-done.1, f32[12,128]{1,0:T(8,128)S(1)} %log_add_fusion, bf16[128,12,128]{0,2,1:T(8,128)(2,1)S(1)} %bitcast.86, bf16[1024,12,128]{0,2,1:T(8,128)(2,1)} %bitcast.83), kind=kOutput, calls=%fused_computation.4 | convolution fusion | flops 407370240 | bytes 16134144 | tf_op jit(solution)/shard_map/qhd,khd->hqk/dot_general | solution.py:73
  185.7 0.0 copy-done.4
  185.7 0.0 slice-done
  185.7 0.0 slice-done.1
  185.7 2.6 multiply_convert_fusion.1
  188.3 37.0 %reduce-scatter.5.cloned.1.call-done = bf16[384,1536]{1,0:T(8,128)(2,1)} async-done(((bf16[1536,1536]{1,0:T(8,128)(2,1)}), bf16[384,1536]{1,0:T(8,128)(2,1)}) %reduce-scatter.5.cloned.1.call-update) | async-done | bytes 1179664 | tf_op jit(solution)/shard_map/reduce_scatter | solution.py:104
  225.3 0.0 all-reduce.3.cloned.1.call-update
  225.3 0.0 copy-start.2
  225.3 0.2 reduce-scatter.3.cloned.1.call-start
  225.6 5.9 %convolution_convert_fusion.2 = bf16[12,128,1024]{2,1,0:T(8,128)(2,1)} fusion(bf16[128,12,128]{0,2,1:T(8,128)(2,1)} %bitcast.87, f32[12,128,1024]{2,1,0:T(8,128)} %copy-done.1, f32[12,128]{1,0:T(8,128)S(1)} %log_add_fusion), kind=kOutput, calls=%fused_computation.13 | convolution fusion | flops 407371776 | bytes 9836544 | tf_op jit(solution)/shard_map/hqk,qhd->khd/dot_general | solution.py:87
  231.4 4.9 %copy.34 = bf16[1024,1536]{1,0:T(8,128)(2,1)} copy(bf16[1024,1536]{0,1:T(8,128)(2,1)} %bitcast.85) | data formatting | bytes 6291456 | tf_op jit(solution)/shard_map/reshape | solution.py:94
  236.3 0.0 copy-done.2
  236.3 3.7 multiply_convert_fusion
  240.0 4.7 %copy.33 = bf16[1024,1536]{1,0:T(8,128)(2,1)} copy(bf16[1024,1536]{0,1:T(8,128)(2,1)} %bitcast.84) | data formatting | bytes 6291456 | tf_op jit(solution)/shard_map/reshape | solution.py:93
  244.7 6.2 %pad_maximum_fusion = bf16[1024,3072]{1,0:T(8,128)(2,1)} fusion(bf16[1024,1536]{1,0:T(8,128)(2,1)} %copy.34, bf16[1024,1536]{1,0:T(8,128)(2,1)} %copy.33), kind=kLoop, calls=%fused_computation.1 | loop fusion | flops 12582912 | bytes 12582912 | tf_op jit(solution)/shard_map/concatenate | solution.py:91
  250.9 0.0 reduce-scatter.3.cloned.1.call-update
  250.9 1.9 copy.29
  252.8 3.6 fusion.3
  256.4 1.9 copy.35
  258.4 4.1 fusion.2
  262.4 46.7 %all-reduce.3.cloned.1.call-done = bf16[384,1536]{1,0:T(8,128)(2,1)} async-done(((bf16[384,1536]{1,0:T(8,128)(2,1)}), bf16[384,1536]{1,0:T(8,128)(2,1)}) %all-reduce.3.cloned.1.call-update) | async-done | bytes 1179664 | tf_op jit(solution)/shard_map/psum | solution.py:112
  309.1 3.0 convert_element_type.65
  312.1 117.8 %reduce-scatter.3.cloned.1.call-done = bf16[128,3072]{1,0:T(8,128)(2,1)} async-done(((bf16[1024,3072]{1,0:T(8,128)(2,1)}), bf16[128,3072]{1,0:T(8,128)(2,1)}) %reduce-scatter.3.cloned.1.call-update) | async-done | bytes 786448 | tf_op jit(solution)/shard_map/reduce_scatter | solution.py:90
  429.8 2.0 slice_bitcast_fusion
  (5 shorter events, 0.0 us)
Async XLA Ops:
  7.2 138.3 %copy-start = (bf16[1,128,1536]{2,1,0:T(8,128)(2,1)S(1)}, bf16[1,128,1536]{2,1,0:T(8,128)(2,1)}, u32[]{:S(2)}) copy-start(bf16[1,128,1536]{2,1,0:T(8,128)(2,1)} %param.15) | copy-start | bytes 1179652
  7.2 130.6 %copy-start.5 = (f32[12]{0:T(128)S(1)}, f32[12]{0:T(128)}, u32[]{:S(2)}) copy-start(f32[12]{0:T(128)} %param.13) | copy-start | bytes 148
  7.2 66.3 %all-gather.6.cloned.1.call-start = ((), (), s32[]{:S(2)}) async-start(), calls=%async_computation.3 | async-start | bytes 3538944 | tf_op jit(solution)/shard_map/all_gather | solution.py:47
  7.9 129.9 %all-gather.4.cloned.1.call-start = ((), (), s32[]{:S(2)}) async-start(), calls=%async_computation.2 | async-start | bytes 3538944 | tf_op jit(solution)/shard_map/all_gather | solution.py:46
  9.9 165.1 %all-gather.8.cloned.1.call-start = ((), (), s32[]{:S(2)}) async-start(), calls=%async_computation.4 | async-start | bytes 5898240 | tf_op jit(solution)/shard_map/all_gather | solution.py:51
  10.6 214.7 %reduce-scatter.5.cloned.1.call-start = ((), (), s32[]{:S(2)}) async-start(), calls=%async_computation.6 | async-start | bytes 5898240 | tf_op jit(solution)/shard_map/reduce_scatter | solution.py:104
  76.6 66.6 %copy-start.3 = (bf16[1,1024,1536]{1,2,0:T(8,128)(2,1)}, bf16[1,1024,1536]{1,2,0:T(8,128)(2,1)S(1)}, u32[]{:S(2)}) copy-start(bf16[1,1024,1536]{1,2,0:T(8,128)(2,1)S(1)} %copy.28) | copy-start | bytes 9437188
  141.8 3.7 copy-start.1
  149.0 160.0 %all-reduce.3.cloned.1.call-start = ((), (), s32[]{:S(2)}) async-start(), calls=%async_computation.7 | async-start | bytes 2359296 | tf_op jit(solution)/shard_map/psum | solution.py:112
  179.0 6.7 %slice-start = ((s8[6291456]{0:T(1024)(128)(4,1)}), s8[2097152]{0:T(1024)(128)(4,1)S(1)}, s32[]{:S(2)}) async-start(s8[6291456]{0:T(1024)(128)(4,1)} %bitcast.80), calls=%async_computation.8 | async-start | bytes 4194304
  179.3 6.4 %copy-start.4 = (bf16[128,1536]{0,1:T(8,128)(2,1)}, bf16[128,1536]{0,1:T(8,128)(2,1)S(1)}, u32[]{:S(2)}) copy-start(bf16[128,1536]{0,1:T(8,128)(2,1)S(1)} %copy.30) | copy-start | bytes 1179652
  179.3 6.4 %slice-start.1 = ((s8[6291456]{0:T(1024)(128)(4,1)}), s8[4194304]{0:T(1024)(128)(4,1)S(1)}, s32[]{:S(2)}) async-start(s8[6291456]{0:T(1024)(128)(4,1)} %bitcast.80), calls=%async_computation.9 | async-start | bytes 8388608
  225.3 11.0 %copy-start.2 = (bf16[12,128,1024]{2,1,0:T(8,128)(2,1)S(1)}, bf16[12,128,1024]{2,1,0:T(8,128)(2,1)}, u32[]{:S(2)}) copy-start(bf16[12,128,1024]{2,1,0:T(8,128)(2,1)} %multiply_convert_fusion.1) | copy-start | bytes 9437188
  225.3 204.5 %reduce-scatter.3.cloned.1.call-start = ((), (), s32[]{:S(2)}) async-start(), calls=%async_computation.5 | async-start | bytes 7077888 | tf_op jit(solution)/shard_map/reduce_scatter | solution.py:90
Sparse Core Ops, SparseCore 0:
  10.2 63.2 all-gather.5
  76.1 61.6 all-gather.3
  139.4 35.6 all-gather.7
  177.4 47.8 reduce-scatter.4
  229.0 79.9 all-reduce.2
  312.5 117.2 reduce-scatter.2
where the time goes:
time: 439 us
  waiting for transfers between devices  315 us (72%)
  matrix products  37.3 us (8%)
  blocking collectives  31 us (7%)
  local copies, waits for them, and re-layouts  24.6 us (6%)
  other arithmetic  15.2 us (3%)
  between operations  14.9 us (3%)
    reduce_scatter x1, waiting for transfers between devices, body(): lax.psum_scatter(jnp.concatenate([key_part.reshape(slot_count * lax.axis_...  118 us
    all_gather x1, waiting for transfers between devices, body(): lax.all_gather(key_rows, 'blk', axis=1, tiled=True)  61.1 us
    psum x1, waiting for transfers between devices, body(): grad_weight = lax.psum(weight_share, 'blk').astype(jnp.float32)  46.7 us
    reduce_scatter x1, waiting for transfers between devices, body(): lax.psum_scatter(jnp.einsum('qi,qo->io', attended, out_grad[0], preferred...  37 us
    all_gather x1, waiting for transfers between devices, body(): weight_all = lax.all_gather(out_weight, 'wide', axis=0, tiled=True)  25.9 us
    all_gather x1, waiting for transfers between devices, body(): lax.all_gather(value_rows, 'blk', axis=1, tiled=True)  25.3 us
    all_gather x1, blocking collectives, body(): lax.all_gather(patch_index, 'blk', axis=1, tiled=True)  17.8 us
    unnamed x1, blocking collectives  13.2 us
  transfers between devices with their start and end apart: 6, of which 6 were waited for; matrix products, arithmetic and copies ran while one was open for 17% of the time, Pallas kernels for 0%

commit v1 on v0

v1 whole, which is shorter than its diff:
```python
import functools
import math

import jax
import jax.numpy as jnp
from jax import lax
from jax.experimental import pallas as pl
from jax.experimental.pallas import tpu as pltpu
from jax.sharding import PartitionSpec as P

HEADS = 12
HEAD_DIM = 128
SIDE = 32
FAR = 1e32
MESH = pl.DeviceIdType.MESH
BF = jnp.bfloat16
F32 = jnp.float32


def dot(a, b, ca, cb):
    return lax.dot_general(a, b, (((ca,), (cb,)), ((), ())), preferred_element_type=F32)


def kernel(
    n, m, G, slopes_ref, aux_ref, q_ref, k_ref, v_ref, w_ref, do_ref,
    lo_ref, dq_ref, dk_ref, dv_ref, gw_ref,
    aux_all, tpad, cols_all, pen, qg, kvg, gg, prob, attg, dqg, acc_k, acc_v,
    dkb, dkin, dkz, do_w, w_all, ga_out, ga_in, ga_full, att_full, att_parts, att_w, lo_acc,
    gwf, gwb, gs, gw_in, gz, gz_in, gout, send_sem, recv_sem,
):
    R = n // G
    H = HEADS // G
    D = HEAD_DIM
    S = q_ref.shape[0]
    wr = w_ref.shape[0]
    rows = wr // n
    scale = HEAD_DIM ** -0.5
    b = lax.axis_index("blk")
    w = lax.axis_index("wide")
    g = b // R
    r = b % R
    sent = []

    def put(src, dst, **device):
        i = len(sent)
        copy = pltpu.make_async_remote_copy(
            src_ref=src, dst_ref=dst, send_sem=send_sem.at[i], recv_sem=recv_sem.at[i],
            device_id=device, device_id_type=MESH,
        )
        copy.start()
        sent.append(copy)
        return copy

    def group(i):
        return (g + i) % G

    def lanes(group_index, h):
        return pl.ds(pl.multiple_of((group_index * H + h) * D, D), D)

    barrier = pltpu.get_barrier_semaphore()
    for i in range(1, n):
        pl.semaphore_signal(barrier, inc=1, device_id={"blk": (b + i) % n}, device_id_type=MESH)
    for i in range(1, m):
        pl.semaphore_signal(barrier, inc=1, device_id={"wide": (w + i) % m}, device_id_type=MESH)
    pl.semaphore_wait(barrier, n + m - 2)

    c_do = [put(do_ref, do_w.at[w], wide=(w + i) % m) for i in range(1, m)]
    c_aux = [put(aux_ref, aux_all.at[b], blk=(b + i) % n) for i in range(1, n)]
    c_kv, c_q = [], []
    for h in range(H):
        for i in range(1, G):
            there = group(i)
            peer = there * R + r
            c_kv.append((h, i, put(k_ref.at[:, lanes(there, h)], kvg.at[h, b, 0], blk=peer)))
            c_kv.append((h, i, put(v_ref.at[:, lanes(there, h)], kvg.at[h, b, 1], blk=peer)))
            c_q.append((h, put(q_ref.at[:, lanes(there, h)], qg.at[h, g], blk=peer)))

    c_fwd = {h: [] for h in range(H)}
    for h in range(H):
        kvg[h, b, 0] = k_ref[:, lanes(g, h)]
        kvg[h, b, 1] = v_ref[:, lanes(g, h)]
        qg[h, g] = q_ref[:, lanes(g, h)]
        for j in range(1, R):
            c_fwd[h].append(put(kvg.at[h, b], kvg.at[h, b], blk=g * R + (r + j) % R))
    do_w[w] = do_ref[...]
    w_all[w] = w_ref[...]
    aux_all[b] = aux_ref[...]

    for c in c_do:
        c.wait_recv()

    def ga_step(c, carry):
        ga_out[c] = dot(do_w[c], w_ref[...], 1, 1).astype(BF)
        return carry

    lax.fori_loop(0, m, ga_step, 0)
    c_ga = [put(ga_out.at[(w + i) % m], ga_in.at[w], wide=(w + i) % m) for i in range(1, m)]
    ga_in[w] = ga_out[w]
    c_w = [put(w_ref, w_all.at[w], wide=(w + i) % m) for i in range(1, m)]

    for c in c_aux:
        c.wait_recv()
    tpad[...] = jnp.zeros_like(tpad)

    def col_step(s, carry):
        tpad[0:8, :] = aux_all[s]
        cols_all[pl.ds(pl.multiple_of(s * S, S), S), :] = tpad[...].T
        return carry

    lax.fori_loop(0, n, col_step, 0)

    def pen_step(t, carry):
        row = aux_all[t * R + r]

        def one(s, inner):
            here = pl.ds(pl.multiple_of(s * S, S), S)
            col = cols_all[here, :]
            far = (
                jnp.abs(col[:, 0:1] - row[0:1, :])
                + jnp.abs(col[:, 1:2] - row[1:2, :])
                + jnp.abs(col[:, 2:3] - row[2:3, :])
            )
            pen[t, here, :] = jnp.where(col[:, 3:4] > 0.5, far, FAR)
            return inner

        lax.fori_loop(0, n, one, 0)
        return carry

    lax.fori_loop(0, G, pen_step, 0)

    def live_rows(t):
        start = pl.multiple_of((t * R + r) * S, S)
        return cols_all[pl.ds(start, S), :][:, 3:4] > 0.5

    def forward_kv(h):
        for hh, i, c in c_kv:
            if hh == h:
                c.wait_recv()
        for i in range(1, G):
            slab = ((g + G - i) % G) * R + r
            for j in range(1, R):
                c_fwd[h].append(put(kvg.at[h, slab], kvg.at[h, slab], blk=g * R + (r + j) % R))

    def fwd(h):
        for c in c_fwd[h]:
            c.wait_recv()
        for hh, c in c_q:
            if hh == h:
                c.wait_recv()
        slope = slopes_ref[g * H + h]

        def step(t, carry):
            s = dot(kvg[h, :, 0].reshape(n * S, D), qg[h, t], 1, 1) * scale - slope * pen[t]
            p = jnp.exp(s - jnp.max(s, axis=0, keepdims=True))
            p = p * (1.0 / jnp.sum(p, axis=0, keepdims=True))
            prob[h, t] = p
            att = dot(p.astype(BF), kvg[h, :, 1].reshape(n * S, D), 0, 0)
            attg[h, t] = jnp.where(live_rows(t), att, 0.0).astype(BF)
            return carry

        lax.fori_loop(0, G, step, 0)
        att_full[:, lanes(g, h)] = attg[h, g]
        return [
            put(attg.at[h, group(i)], att_full.at[:, lanes(g, h)], blk=group(i) * R + r)
            for i in range(1, G)
        ]

    forward_kv(0)

    for c in c_ga:
        c.wait_recv()
    for i in range(m):
        ga_full[:, i * wr : (i + 1) * wr] = ga_in[i]
    c_gg = {h: [] for h in range(H)}
    for h in range(H):
        gg[h, g] = ga_full[:, lanes(g, h)]
        for i in range(1, G):
            c_gg[h].append(
                put(ga_full.at[:, lanes(group(i), h)], gg.at[h, g], blk=group(i) * R + r)
            )

    c_att = []
    for h in range(H):
        if h + 1 < H:
            forward_kv(h + 1)
        c_att += fwd(h)

    c_dq, c_dk, c_dz = [], {}, []

    def bwd(h):
        for c in c_gg[h]:
            c.wait_recv()
        acc_k[h] = jnp.zeros((n * S, D), F32)
        acc_v[h] = jnp.zeros((n * S, D), F32)

        def step(t, carry):
            ga = gg[h, t]
            ga = jnp.where(live_rows(t), ga.astype(F32), 0.0).astype(BF)
            p = prob[h, t]
            gp = dot(kvg[h, :, 1].reshape(n * S, D), ga, 1, 1)
            delta = jnp.sum(p * gp, axis=0, keepdims=True)
            gs = (p * (gp - delta)).astype(BF)
            dqg[h, t] = (dot(gs, kvg[h, :, 0].reshape(n * S, D), 0, 0) * scale).astype(BF)
            acc_k[h] += dot(gs, qg[h, t], 1, 0) * scale
            acc_v[h] += dot(p.astype(BF), ga, 1, 0)
            return carry

        lax.fori_loop(0, G, step, 0)
        for rr in range(R):
            for t in range(G):
                at = (t * R + rr) * S
                dkb[h, rr, 0, t] = acc_k[h, at : at + S, :].astype(BF)
                dkb[h, rr, 1, t] = acc_v[h, at : at + S, :].astype(BF)
        c_dk[h] = [
            put(dkb.at[h, (r + j) % R], dkin.at[h, r], blk=g * R + (r + j) % R)
            for j in range(1, R)
        ]
        dq_ref[:, lanes(g, h)] = dqg[h, g]
        for i in range(1, G):
            c_dq.append(
                put(dqg.at[h, group(i)], dq_ref.at[:, lanes(g, h)], blk=group(i) * R + r)
            )

    def finish_keys(h):
        for c in c_dk[h]:
            c.wait_recv()

        def step(t, carry):
            here = pl.ds(pl.multiple_of((t * R + r) * S, S), S)
            total_k = acc_k[h, here, :]
            total_v = acc_v[h, here, :]
            for j in range(1, R):
                total_k += dkin[h, (r + j) % R, 0, t].astype(F32)
                total_v += dkin[h, (r + j) % R, 1, t].astype(F32)
            dkz[h, 0, t] = total_k.astype(BF)
            dkz[h, 1, t] = total_v.astype(BF)
            return carry

        lax.fori_loop(0, G, step, 0)
        dk_ref[:, lanes(g, h)] = dkz[h, 0, g]
        dv_ref[:, lanes(g, h)] = dkz[h, 1, g]
        for i in range(1, G):
            peer = group(i) * R + r
            c_dz.append(put(dkz.at[h, 0, group(i)], dk_ref.at[:, lanes(g, h)], blk=peer))
            c_dz.append(put(dkz.at[h, 1, group(i)], dv_ref.at[:, lanes(g, h)], blk=peer))

    bwd(0)

    for c in c_att:
        c.wait_recv()
    for i in range(m):
        att_parts[i] = att_full[:, i * wr : (i + 1) * wr]
    c_aw = [put(att_parts.at[(w + i) % m], att_w.at[w], wide=(w + i) % m) for i in range(1, m)]
    att_w[w] = att_parts[w]

    bwd(1)
    finish_keys(0)

    for c in c_aw:
        c.wait_recv()
    width = do_ref.shape[1]
    chunk = 512

    def gw_step(s, carry):
        here = pl.ds(pl.multiple_of(s * chunk, chunk), chunk)
        gwf[:, here] = dot(att_w[...].reshape(m * S, wr), do_w[:, :, here].reshape(m * S, chunk), 0, 0)
        return carry

    lax.fori_loop(0, width // chunk, gw_step, 0)
    for rr in range(R):
        for t in range(G):
            at = (rr * G + t) * rows
            gwb[rr, t] = gwf[at : at + rows, :]
    c_g1 = []
    for j in range(1, R):
        there = (r + j) % R
        gs[there] = gwb[there].astype(BF)
        c_g1.append(put(gs.at[there], gw_in.at[r], blk=g * R + there))

    for h in range(2, H):
        bwd(h)
        finish_keys(h - 1)

    for c in c_g1:
        c.wait_recv()

    def g1_step(t, carry):
        total = gwb[r, t]
        for j in range(1, R):
            total += gw_in[(r + j) % R, t].astype(F32)
        gz[t] = total.astype(BF)
        return carry

    lax.fori_loop(0, G, g1_step, 0)
    c_g2 = [put(gz.at[group(i)], gz_in.at[g], blk=group(i) * R + r) for i in range(1, G)]
    finish_keys(H - 1)

    for c in c_w:
        c.wait_recv()
    lo_acc[...] = jnp.zeros_like(lo_acc)

    def lo_step(i, carry):
        lo_acc[...] += dot(att_parts[i], w_all[i], 1, 0)
        return carry

    lax.fori_loop(0, m, lo_step, 0)
    lo_ref[...] = lo_acc[...].astype(BF)

    for c in c_g2:
        c.wait_recv()
    total = gz[g].astype(F32)
    for i in range(1, G):
        total += gz_in[group(i)].astype(F32)
    gout[r, g] = total.astype(BF)
    c_g3 = [put(gout.at[r, g], gout.at[r, g], blk=group(i) * R + r) for i in range(1, G)]
    for c in c_g3:
        c.wait_recv()
    c_g4 = [put(gout.at[r], gout.at[r], blk=g * R + (r + j) % R) for j in range(1, R)]
    for c in c_g4:
        c.wait_recv()
    for rr in range(R):
        for t in range(G):
            at = (rr * G + t) * rows
            gw_ref[at : at + rows, :] = gout[rr, t].astype(F32)
    for c in c_dq + c_dz:
        c.wait_recv()
    for c in sent:
        c.wait_send()


def body(query_rows, key_rows, value_rows, patch_index, live_count, slopes, out_weight, out_grad):
    n = lax.axis_size("blk")
    m = lax.axis_size("wide")
    G = math.gcd(HEADS, n)
    R = n // G
    H = HEADS // G
    S, inner = query_rows.shape[1:]
    wr, width = out_weight.shape
    rows = wr // n
    D = HEAD_DIM
    index = patch_index[0]
    live = jnp.arange(S, dtype=jnp.int32) < live_count[0, 0]
    zero = jnp.zeros((S,), jnp.int32)
    aux = jnp.stack(
        [index % SIDE, index // SIDE % SIDE, index // (SIDE * SIDE), live.astype(jnp.int32)] + [zero] * 4
    ).astype(F32)
    per = 2 * H * (G - 1) + H * (G - 1)
    copies = (
        3 * (m - 1) + (n - 1) + per + H * G * (R - 1) + H * (G - 1) * 5 + H * (R - 1)
        + (m - 1) + 2 * (R - 1) + 2 * (G - 1)
    )
    vmem = pl.BlockSpec(memory_space=pltpu.VMEM)
    outs = pl.pallas_call(
        functools.partial(kernel, n, m, G),
        out_shape=[jax.ShapeDtypeStruct((S, inner), BF)] * 4 + [jax.ShapeDtypeStruct((wr, width), F32)],
        in_specs=[pl.BlockSpec(memory_space=pltpu.SMEM)] + [vmem] * 6,
        out_specs=[vmem] * 5,
        scratch_shapes=[
            pltpu.VMEM((n, 8, S), F32),
            pltpu.VMEM((128, S), F32),
            pltpu.VMEM((n * S, 128), F32),
            pltpu.VMEM((G, n * S, S), F32),
            pltpu.VMEM((H, G, S, D), BF),
            pltpu.VMEM((H, n, 2, S, D), BF),
            pltpu.VMEM((H, G, S, D), BF),
            pltpu.VMEM((H, G, n * S, S), F32),
            pltpu.VMEM((H, G, S, D), BF),
            pltpu.VMEM((H, G, S, D), BF),
            pltpu.VMEM((H, n * S, D), F32),
            pltpu.VMEM((H, n * S, D), F32),
            pltpu.VMEM((H, R, 2, G, S, D), BF),
            pltpu.VMEM((H, R, 2, G, S, D), BF),
            pltpu.VMEM((H, 2, G, S, D), BF),
            pltpu.VMEM((m, S, width), BF),
            pltpu.VMEM((m, wr, width), BF),
            pltpu.VMEM((m, S, wr), BF),
            pltpu.VMEM((m, S, wr), BF),
            pltpu.VMEM((S, inner), BF),
            pltpu.VMEM((S, inner), BF),
            pltpu.VMEM((m, S, wr), BF),
            pltpu.VMEM((m, S, wr), BF),
            pltpu.VMEM((S, width), F32),
            pltpu.VMEM((wr, width), F32),
            pltpu.VMEM((R, G, rows, width), F32),
            pltpu.VMEM((R, G, rows, width), BF),
            pltpu.VMEM((R, G, rows, width), BF),
            pltpu.VMEM((G, rows, width), BF),
            pltpu.VMEM((G, rows, width), BF),
            pltpu.VMEM((R, G, rows, width), BF),
            pltpu.SemaphoreType.DMA((copies,)),
            pltpu.SemaphoreType.DMA((copies,)),
        ],
        compiler_params=pltpu.CompilerParams(
            collective_id=0, has_side_effects=True, vmem_limit_bytes=56 * 1024 * 1024
        ),
    )(slopes, aux, query_rows[0], key_rows[0], value_rows[0], out_weight, out_grad[0])
    return outs[0][None], outs[1][None], outs[2][None], outs[3][None], outs[4]


def solution(mesh):
    rows = P("wide", "blk", None)
    placed = (rows, rows, rows, P("wide", "blk"), P("wide", "blk"), P(), P("wide", None), rows)
    return jax.shard_map(
        body,
        mesh=mesh,
        in_specs=placed,
        out_specs=(rows, rows, rows, rows, P("wide", None)),
        check_vma=False,
    )
```

time: 439 us -> 162 us (0.37)
  waiting for transfers between devices: 315 us -> 0 us
  Pallas kernels: 0 us -> 150 us
  matrix products: 37.3 us -> 0 us
  blocking collectives: 31 us -> 0 us
  local copies, waits for them, and re-layouts: 24.6 us -> 8.65 us
  other arithmetic: 15.2 us -> 1.28 us
  between operations: 14.9 us -> 1.31 us
    reduce_scatter x2 -> x0, waiting for transfers between devices: 155 us -> none  [the longest x1 118 us: body(): lax.psum_scatter(jnp.concatenate([key_part.reshape(slot_count * lax.axis_...]
    pallas_call x0 -> x1, Pallas kernels: none -> 150 us  [body(): pl.pallas_call(functools.partial(kernel, n, m, G), out_shape=[jax.ShapeDt...]
    all_gather x3 -> x0, waiting for transfers between devices: 112 us -> none  [the longest x1 61.1 us: body(): lax.all_gather(key_rows, 'blk', axis=1, tiled=True)]
    psum x1 -> x0, waiting for transfers between devices: 46.7 us -> none  [body(): grad_weight = lax.psum(weight_share, 'blk').astype(jnp.float32)]
    dot_general x9 -> x0, matrix products: 37.3 us -> none  [the longest x1 6.4 us: body(): jnp.einsum('qhd,khd->hqk', grad_heads, value_heads, preferred_element_typ...]
    all_gather x1 -> x0, blocking collectives: 17.8 us -> none  [body(): lax.all_gather(patch_index, 'blk', axis=1, tiled=True)]
    unnamed x1 -> x0, blocking collectives: 13.2 us -> none
    reshape x3 -> x0, local copies, waits for them, and re-layouts: 11.4 us -> none  [the longest x1 4.85 us: body(): value_part.reshape(slot_count * lax.axis_size('blk'), inner_width)]
  transfers between devices with their start and end apart: 6 -> 0, of which waited for: 6 -> 0; matrix products, arithmetic and copies ran while one was open for 17% -> 0% of each run, Pallas kernels for 0% -> 0%
where the time goes in v1:
time: 162 us; the launch traced here: 161 us
  Pallas kernels  150 us (93%)
  local copies, waits for them, and re-layouts  8.65 us (5%)
    pallas_call x1, Pallas kernels, body(): pl.pallas_call(functools.partial(kernel, n, m, G), out_shape=[jax.ShapeDt...  150 us
    unnamed x7, local copies, waits for them, and re-layouts  8.62 us

profile of v1, /device:TPU:0, one launch (start us, length us, event | category | flops | bytes accessed | tf_op | source)
XLA Modules:
  0.0 160.8 jit_solution(10624334281340234239)
XLA Ops:
  1.3 0.7 and_select_fusion
  2.0 0.6 convert_element_type.14.aux_ref
  2.6 149.6 %shard_map.119 = (bf16[128,1536]{1,0:T(8,128)(2,1)}, bf16[128,1536]{1,0:T(8,128)(2,1)}, bf16[128,1536]{1,0:T(8,128)(2,1)}, bf16[128,1536]{1,0:T(8,128)(2,1)}, f32[384,1536]{1,0:T(8,128)}) custom-call(f32[12]{0:T(128)} %slopes_ref.1, f32[8,128]{1,0:T(8,128)} %convert_element_type.14.aux_ref, bf16[128,1536]{1,0:T(8,128)(2,1)} %bitcast.10, ...), custom_call_target="tpu_custom_call" | custom-call | tf_op jit(solution)/shard_map/pallas_call | solution.py:353
  152.2 0.0 copy-start
  152.2 1.9 %copy.19 = bf16[1,128,1536]{2,1,0:T(8,128)(2,1)} copy(bf16[1,128,1536]{2,1,0:T(8,128)(2,1)} %bitcast.17) | data formatting | bytes 786432
  154.1 1.8 %copy.20 = bf16[1,128,1536]{2,1,0:T(8,128)(2,1)} copy(bf16[1,128,1536]{2,1,0:T(8,128)(2,1)} %bitcast.16) | data formatting | bytes 786432
  155.9 1.8 %copy.21 = bf16[1,128,1536]{2,1,0:T(8,128)(2,1)} copy(bf16[1,128,1536]{2,1,0:T(8,128)(2,1)} %bitcast.15) | data formatting | bytes 786432
  157.6 1.8 %copy.22 = bf16[1,128,1536]{2,1,0:T(8,128)(2,1)} copy(bf16[1,128,1536]{2,1,0:T(8,128)(2,1)} %bitcast.14) | data formatting | bytes 786432
  159.4 0.0 copy-done
  159.4 1.4 copy.23
  (3 shorter events, 0.0 us)
Async XLA Ops:
  152.2 7.2 %copy-start = (f32[384,1536]{1,0:T(8,128)S(1)}, f32[384,1536]{1,0:T(8,128)}, u32[]{:S(2)}) copy-start(f32[384,1536]{1,0:T(8,128)} %get-tuple-element.27) | copy-start | bytes 7077892

commit v2 on v1

--- a/solution.py
+++ b/solution.py
@@ -26,7 +26,7 @@
     lo_ref, dq_ref, dk_ref, dv_ref, gw_ref,
     aux_all, tpad, cols_all, pen, qg, kvg, gg, prob, attg, dqg, acc_k, acc_v,
     dkb, dkin, dkz, do_w, w_all, ga_out, ga_in, ga_full, att_full, att_parts, att_w, lo_acc,
-    gwf, gwb, gs, gw_in, gz, gz_in, gout, send_sem, recv_sem,
+    gwb, gs, gw_in, gz, gz_in, gout, send_sem, recv_sem,
 ):
     R = n // G
     H = HEADS // G
@@ -64,7 +64,14 @@
         pl.semaphore_signal(barrier, inc=1, device_id={"wide": (w + i) % m}, device_id_type=MESH)
     pl.semaphore_wait(barrier, n + m - 2)
 
-    c_do = [put(do_ref, do_w.at[w], wide=(w + i) % m) for i in range(1, m)]
+    pairs = m // 2
+    other = (w // 2) * 2 + (w + 1) % 2
+
+    def away(i):
+        return (w + 2 * i) % m
+
+    c_do = [put(do_ref, do_w.at[w], wide=away(i)) for i in range(1, pairs)]
+    c_do2 = [put(do_ref, do_w.at[w], wide=other)]
     c_aux = [put(aux_ref, aux_all.at[b], blk=(b + i) % n) for i in range(1, n)]
     c_kv, c_q = [], []
     for h in range(H):
@@ -86,7 +93,10 @@
     w_all[w] = w_ref[...]
     aux_all[b] = aux_ref[...]
 
-    for c in c_do:
+    for i, c in enumerate(c_do, 1):
+        c.wait_recv()
+        c_do2.append(put(do_w.at[away(pairs - i)], do_w.at[away(pairs - i)], wide=other))
+    for c in c_do2:
         c.wait_recv()
 
     def ga_step(c, carry):
@@ -96,7 +106,8 @@
     lax.fori_loop(0, m, ga_step, 0)
     c_ga = [put(ga_out.at[(w + i) % m], ga_in.at[w], wide=(w + i) % m) for i in range(1, m)]
     ga_in[w] = ga_out[w]
-    c_w = [put(w_ref, w_all.at[w], wide=(w + i) % m) for i in range(1, m)]
+    c_w = [put(w_ref, w_all.at[w], wide=away(i)) for i in range(1, pairs)]
+    c_w2 = [put(w_ref, w_all.at[w], wide=other)]
 
     for c in c_aux:
         c.wait_recv()
@@ -254,48 +265,75 @@
     att_w[w] = att_parts[w]
 
     bwd(1)
+
+    for c in c_aw:
+        c.wait_recv()
+    chunk = gs.shape[-1]
+    chunks = gs.shape[0]
+    c_g1 = []
+    for s in range(chunks):
+        here = slice(s * chunk, (s + 1) * chunk)
+        part = dot(att_w[...].reshape(m * S, wr), do_w[:, :, here].reshape(m * S, chunk), 0, 0)
+        for rr in range(R):
+            for t in range(G):
+                at = (rr * G + t) * rows
+                gwb[s, rr, t] = part[at : at + rows, :]
+        c_g1.append([])
+        for j in range(1, R):
+            there = (r + j) % R
+            gs[s, there] = gwb[s, there].astype(BF)
+            c_g1[s].append(put(gs.at[s, there], gw_in.at[s, r], blk=g * R + there))
+
     finish_keys(0)
-
-    for c in c_aw:
-        c.wait_recv()
-    width = do_ref.shape[1]
-    chunk = 512
-
-    def gw_step(s, carry):
-        here = pl.ds(pl.multiple_of(s * chunk, chunk), chunk)
-        gwf[:, here] = dot(att_w[...].reshape(m * S, wr), do_w[:, :, here].reshape(m * S, chunk), 0, 0)
-        return carry
-
-    lax.fori_loop(0, width // chunk, gw_step, 0)
-    for rr in range(R):
-        for t in range(G):
-            at = (rr * G + t) * rows
-            gwb[rr, t] = gwf[at : at + rows, :]
-    c_g1 = []
-    for j in range(1, R):
-        there = (r + j) % R
-        gs[there] = gwb[there].astype(BF)
-        c_g1.append(put(gs.at[there], gw_in.at[r], blk=g * R + there))
+    for i, c in enumerate(c_w, 1):
+        c.wait_recv()
+        c_w2.append(put(w_all.at[away(pairs - i)], w_all.at[away(pairs - i)], wide=other))
 
     for h in range(2, H):
         bwd(h)
         finish_keys(h - 1)
 
-    for c in c_g1:
-        c.wait_recv()
-
-    def g1_step(t, carry):
-        total = gwb[r, t]
+    c_g2, c_g3, c_g4 = {}, {}, []
+
+    def in_group(s):
+        for c in c_g1[s]:
+            c.wait_recv()
+        total = gwb[s, r]
         for j in range(1, R):
-            total += gw_in[(r + j) % R, t].astype(F32)
-        gz[t] = total.astype(BF)
-        return carry
-
-    lax.fori_loop(0, G, g1_step, 0)
-    c_g2 = [put(gz.at[group(i)], gz_in.at[g], blk=group(i) * R + r) for i in range(1, G)]
-    finish_keys(H - 1)
-
-    for c in c_w:
+            total += gw_in[s, (r + j) % R].astype(F32)
+        gz[s] = total.astype(BF)
+        c_g2[s] = [
+            put(gz.at[s, group(i)], gz_in.at[s, g], blk=group(i) * R + r) for i in range(1, G)
+        ]
+
+    def over_groups(s):
+        for c in c_g2[s]:
+            c.wait_recv()
+        total = gz[s, g].astype(F32)
+        for i in range(1, G):
+            total += gz_in[s, group(i)].astype(F32)
+        gout[s, r, g] = total.astype(BF)
+        c_g3[s] = [
+            put(gout.at[s, r, g], gout.at[s, r, g], blk=group(i) * R + r) for i in range(1, G)
+        ]
+
+    def spread(s):
+        for c in c_g3[s]:
+            c.wait_recv()
+        for j in range(1, R):
+            c_g4.append(put(gout.at[s, r], gout.at[s, r], blk=g * R + (r + j) % R))
+
+    for tick in range(chunks + 2):
+        if tick < chunks:
+            in_group(tick)
+        if 1 <= tick <= chunks:
+            over_groups(tick - 1)
+        if tick == 1:
+            finish_keys(H - 1)
+        if tick >= 2:
+            spread(tick - 2)
+
+    for c in c_w2:
         c.wait_recv()
     lo_acc[...] = jnp.zeros_like(lo_acc)
 
@@ -306,22 +344,13 @@
     lax.fori_loop(0, m, lo_step, 0)
     lo_ref[...] = lo_acc[...].astype(BF)
 
-    for c in c_g2:
-        c.wait_recv()
-    total = gz[g].astype(F32)
-    for i in range(1, G):
-        total += gz_in[group(i)].astype(F32)
-    gout[r, g] = total.astype(BF)
-    c_g3 = [put(gout.at[r, g], gout.at[r, g], blk=group(i) * R + r) for i in range(1, G)]
-    for c in c_g3:
-        c.wait_recv()
-    c_g4 = [put(gout.at[r], gout.at[r], blk=g * R + (r + j) % R) for j in range(1, R)]
     for c in c_g4:
         c.wait_recv()
-    for rr in range(R):
-        for t in range(G):
-            at = (rr * G + t) * rows
-            gw_ref[at : at + rows, :] = gout[rr, t].astype(F32)
+    for s in range(chunks):
+        for rr in range(R):
+            for t in range(G):
+                at = (rr * G + t) * rows
+                gw_ref[at : at + rows, s * chunk : (s + 1) * chunk] = gout[s, rr, t].astype(F32)
     for c in c_dq + c_dz:
         c.wait_recv()
     for c in sent:
@@ -338,6 +367,7 @@
     wr, width = out_weight.shape
     rows = wr // n
     D = HEAD_DIM
+    NC = width // 512
     index = patch_index[0]
     live = jnp.arange(S, dtype=jnp.int32) < live_count[0, 0]
     zero = jnp.zeros((S,), jnp.int32)
@@ -347,7 +377,7 @@
     per = 2 * H * (G - 1) + H * (G - 1)
     copies = (
         3 * (m - 1) + (n - 1) + per + H * G * (R - 1) + H * (G - 1) * 5 + H * (R - 1)
-        + (m - 1) + 2 * (R - 1) + 2 * (G - 1)
+        + (m - 1) + NC * (2 * (R - 1) + 2 * (G - 1))
     )
     vmem = pl.BlockSpec(memory_space=pltpu.VMEM)
     outs = pl.pallas_call(
@@ -380,13 +410,12 @@
             pltpu.VMEM((m, S, wr), BF),
             pltpu.VMEM((m, S, wr), BF),
             pltpu.VMEM((S, width), F32),
-            pltpu.VMEM((wr, width), F32),
-            pltpu.VMEM((R, G, rows, width), F32),
-            pltpu.VMEM((R, G, rows, width), BF),
-            pltpu.VMEM((R, G, rows, width), BF),
-            pltpu.VMEM((G, rows, width), BF),
-            pltpu.VMEM((G, rows, width), BF),
-            pltpu.VMEM((R, G, rows, width), BF),
+            pltpu.VMEM((NC, R, G, rows, width // NC), F32),
+            pltpu.VMEM((NC, R, G, rows, width // NC), BF),
+            pltpu.VMEM((NC, R, G, rows, width // NC), BF),
+            pltpu.VMEM((NC, G, rows, width // NC), BF),
+            pltpu.VMEM((NC, G, rows, width // NC), BF),
+            pltpu.VMEM((NC, R, G, rows, width // NC), BF),
             pltpu.SemaphoreType.DMA((copies,)),
             pltpu.SemaphoreType.DMA((copies,)),
         ],

time: 162 us -> 128 us (0.79)
  Pallas kernels: 150 us -> 117 us
    pallas_call x1, Pallas kernels: 150 us -> 117 us  [body(): pl.pallas_call(functools.partial(kernel, n, m, G), out_shape=[jax.ShapeDt...]
where the time goes in v2:
time: 128 us
  Pallas kernels  117 us (91%)
  local copies, waits for them, and re-layouts  8.65 us (7%)
  between operations  1.31 us (1%)
  other arithmetic  1.28 us (1%)
    pallas_call x1, Pallas kernels, body(): pl.pallas_call(functools.partial(kernel, n, m, G), out_shape=[jax.ShapeDt...  117 us
    unnamed x7, local copies, waits for them, and re-layouts  8.62 us

profile of v2, /device:TPU:0, one launch (start us, length us, event | category | flops | bytes accessed | tf_op | source)
XLA Modules:
  0.0 128.1 jit_solution(16758045195810218521)
XLA Ops:
  1.3 0.7 and_select_fusion
  2.0 0.6 convert_element_type.14.aux_ref
  2.6 116.8 %shard_map.119 = (bf16[128,1536]{1,0:T(8,128)(2,1)}, bf16[128,1536]{1,0:T(8,128)(2,1)}, bf16[128,1536]{1,0:T(8,128)(2,1)}, bf16[128,1536]{1,0:T(8,128)(2,1)}, f32[384,1536]{1,0:T(8,128)}) custom-call(f32[12]{0:T(128)} %slopes_ref.1, f32[8,128]{1,0:T(8,128)} %convert_element_type.14.aux_ref, bf16[128,1536]{1,0:T(8,128)(2,1)} %bitcast.10, ...), custom_call_target="tpu_custom_call" | custom-call | tf_op jit(solution)/shard_map/pallas_call | solution.py:383
  119.5 0.0 copy-start
  119.5 1.9 %copy.19 = bf16[1,128,1536]{2,1,0:T(8,128)(2,1)} copy(bf16[1,128,1536]{2,1,0:T(8,128)(2,1)} %bitcast.17) | data formatting | bytes 786432
  121.4 1.8 %copy.20 = bf16[1,128,1536]{2,1,0:T(8,128)(2,1)} copy(bf16[1,128,1536]{2,1,0:T(8,128)(2,1)} %bitcast.16) | data formatting | bytes 786432
  123.1 1.8 %copy.21 = bf16[1,128,1536]{2,1,0:T(8,128)(2,1)} copy(bf16[1,128,1536]{2,1,0:T(8,128)(2,1)} %bitcast.15) | data formatting | bytes 786432
  124.9 1.8 %copy.22 = bf16[1,128,1536]{2,1,0:T(8,128)(2,1)} copy(bf16[1,128,1536]{2,1,0:T(8,128)(2,1)} %bitcast.14) | data formatting | bytes 786432
  126.7 0.0 copy-done
  126.7 1.4 %copy.23 = f32[384,1536]{1,0:T(8,128)} copy(f32[384,1536]{1,0:T(8,128)S(1)} %copy-done) | data formatting | bytes 4718592
  (3 shorter events, 0.0 us)
Async XLA Ops:
  119.5 7.2 %copy-start = (f32[384,1536]{1,0:T(8,128)S(1)}, f32[384,1536]{1,0:T(8,128)}, u32[]{:S(2)}) copy-start(f32[384,1536]{1,0:T(8,128)} %get-tuple-element.27) | copy-start | bytes 7077892
